TPU v7x, 32 devices: a whole 2x2x4 slice. The times are simulated.
32 devices in a mesh: date: 2 (over y), slab: 16 (over z, x, core).
Axes of the slice: x: 2, y: 2, z: 4, core: 2. Of those that a mesh axis runs over, the one named last changes fastest.
Arguments:
- pressure: float32 [16, 12288], P('slab', 'date'), parts along dimension 1, may hold values from -6 to 6
- density: float32 [16, 12288], P('slab', 'date'), parts along dimension 1, may hold values from -6 to 6
- vertical_wind: float32 [16, 12288], P('slab', 'date'), parts along dimension 1, may hold values from -6 to 6
- horizontal_wind: float32 [2, 16, 12288], P(None, 'slab', 'date'), parts along dimension 2, may hold values from -6 to 6
- metric_terms: float32 [2, 6144], replicated, may hold values from 0.25 to 1
- neighbors: int32 [4, 6144], replicated, may hold values from 0 to 6143, as said below
- level_order: int32 [16], replicated, may hold values from 0 to 15, each once
- stiffness: float32 [16], replicated, may hold values from 0.2 to 5
- coupling: float32 [16], replicated, may hold values from 0.2 to 1
- weight_one: bfloat16 [64, 512], P('slab'), may hold values from -0.75 to 0.75
- weight_two: bfloat16 [512, 512], P('slab'), may hold values from -0.25 to 0.25
- weight_three: bfloat16 [512, 16], P('slab'), may hold values from -0.25 to 0.25
- pressure_adjoint: float32 [16, 12288], P('slab', 'date'), parts along dimension 1, may hold values from -6 to 6
- wind_adjoint: float32 [16, 12288], P('slab', 'date'), parts along dimension 1, may hold values from -6 to 6
Outputs:
- pressure_new: float32 [16, 12288], P('slab', 'date'), parts along dimension 1
- wind_new: float32 [16, 12288], P('slab', 'date'), parts along dimension 1
- pressure_grad: float32 [16, 12288], P('slab', 'date'), parts along dimension 1
- first_grad: float32 [128, 512], P(('date', 'slab')), parts along dimension 0
- second_grad: float32 [1024, 512], P(('date', 'slab')), parts along dimension 0
- third_grad: float32 [1024, 16], P(('date', 'slab')), parts along dimension 0
There are 2 independent parts, one for each index of `date`. A program takes and returns all parts, laid end to end along the dimension named above; an argument that names none is the same for every part. Nothing has to cross between parts.
Inputs may be any that keep to these rules, and one draw needn't show every extreme that they name: `neighbors`: the columns are the cells of a 8 x 768 grid stored in some order; rows 0, 1, 2, 3 give the stored positions of a column's east, west, north and south neighbours, and the column itself where the grid's edge lies on that side. `level_order`: each level appears once.
All inputs are finite; a program needn't handle non-finite values.
Results may differ from a plain program's by a relative error of at most 0.0075.
Values may be sent and summed in bfloat16 or wider, within the bound.
No kernel may reach another device: no remote copies, remote signals or barrier semaphores. Data moves between devices by JAX's collectives and lax.ppermute only.
A program may use at most 128 MiB of HBM per device.

v0:
```python
import math
import jax
import jax.numpy as jnp
from jax import lax
from jax.sharding import PartitionSpec as P


def lower_diff(field):
    return jnp.concatenate([field[1:] - field[:-1], -field[-1:]], axis=0)


def upper_diff(field):
    return jnp.concatenate([jnp.zeros_like(field[:1]), field[:-1]], axis=0) - field


def level_inverse(stiffness):
    below = jnp.concatenate([jnp.zeros((1,), jnp.float32), stiffness[:-1]])
    matrix = (
        jnp.diag(1.0 + stiffness + below)
        - jnp.diag(stiffness[:-1], 1)
        - jnp.diag(stiffness[:-1], -1)
    )
    factor = jnp.linalg.cholesky(matrix)
    identity = jnp.eye(stiffness.shape[0], dtype=jnp.float32)
    return jax.scipy.linalg.cho_solve((factor, True), identity)


def apply_inverse(inverse_matrix, rhs):
    return jnp.dot(
        inverse_matrix, rhs, precision=lax.Precision.HIGHEST, preferred_element_type=jnp.float32
    )


def contract_first(left, right):
    return lax.dot_general(
        left, right, (((0,), (0,)), ((), ())), preferred_element_type=jnp.float32
    )


def contract_last(left, right):
    return lax.dot_general(
        left, right, (((1,), (1,)), ((), ())), preferred_element_type=jnp.float32
    )


def body(
    pressure,
    density,
    vertical_wind,
    horizontal_wind,
    metric_terms,
    neighbors,
    level_order,
    stiffness,
    coupling,
    weight_one,
    weight_two,
    weight_three,
    pressure_adjoint,
    wind_adjoint,
):
    east = jnp.take(horizontal_wind[0], neighbors[0], axis=1)
    west = jnp.take(horizontal_wind[0], neighbors[1], axis=1)
    north = jnp.take(horizontal_wind[1], neighbors[2], axis=1)
    south = jnp.take(horizontal_wind[1], neighbors[3], axis=1)
    diverg = metric_terms[0] * (east - west) + metric_terms[1] * (north - south)
    star = pressure - diverg
    inverse = jnp.argsort(level_order)
    scale = 1.0 / math.sqrt(neighbors.shape[1])
    forward_raw = lax.all_to_all(
        jnp.stack([star, density, vertical_wind, diverg]).astype(jnp.bfloat16),
        "slab",
        split_axis=2,
        concat_axis=1,
        tiled=True,
    ).astype(jnp.float32)
    full_one, full_two, full_three = (
        lax.all_gather(weight_one, "slab", axis=0, tiled=True),
        lax.all_gather(weight_two, "slab", axis=0, tiled=True),
        lax.all_gather(weight_three, "slab", axis=0, tiled=True),
    )
    forward_part = jnp.take(forward_raw, inverse, axis=1)
    levels = forward_part.shape[1]
    width = forward_part.shape[2]
    couple = coupling[:, None]
    column_input = forward_part.reshape(4 * levels, width).astype(jnp.bfloat16)
    pre_one = contract_first(full_one, column_input)
    tanh_one = jnp.tanh(pre_one)
    act_one = tanh_one.astype(jnp.bfloat16)
    pre_two = contract_first(full_two, act_one)
    tanh_two = jnp.tanh(pre_two)
    act_two = tanh_two.astype(jnp.bfloat16)
    heating = contract_first(full_three, act_two)
    star_column = forward_part[0]
    rhs = forward_part[2] - couple * lower_diff(star_column) - 0.5 * forward_part[1] + heating
    inverse_matrix = level_inverse(stiffness)
    wind_next = apply_inverse(inverse_matrix, rhs)
    press_next = star_column + upper_diff(couple * wind_next)
    forward_slabs = lax.all_to_all(
        jnp.take(jnp.stack([press_next, wind_next]), level_order, axis=1).astype(jnp.bfloat16),
        "slab",
        split_axis=1,
        concat_axis=2,
        tiled=True,
    ).astype(jnp.float32)
    adjoint_raw = lax.all_to_all(
        jnp.stack([pressure_adjoint, wind_adjoint]), "slab", split_axis=2, concat_axis=1, tiled=True
    )
    adjoint_part = jnp.take(adjoint_raw, inverse, axis=1)
    wind_grad = adjoint_part[1] + couple * lower_diff(adjoint_part[0])
    rhs_grad = apply_inverse(inverse_matrix, wind_grad)
    star_grad = adjoint_part[0] - upper_diff(couple * rhs_grad)
    heat_grad = rhs_grad.astype(jnp.bfloat16)
    local_three = contract_last(act_two, heat_grad) * scale
    back_two = jnp.dot(full_three, heat_grad, preferred_element_type=jnp.float32)
    pre_two_grad = (back_two * (1.0 - tanh_two * tanh_two)).astype(jnp.bfloat16)
    local_two = contract_last(act_one, pre_two_grad) * scale
    back_one = jnp.dot(full_two, pre_two_grad, preferred_element_type=jnp.float32)
    pre_one_grad = (back_one * (1.0 - tanh_one * tanh_one)).astype(jnp.bfloat16)
    local_one = contract_last(column_input, pre_one_grad) * scale
    first_grad, second_grad, third_grad = (
        lax.psum_scatter(local_one, "slab", scatter_dimension=0, tiled=True),
        lax.psum_scatter(local_two, "slab", scatter_dimension=0, tiled=True),
        lax.psum_scatter(local_three, "slab", scatter_dimension=0, tiled=True),
    )
    input_grad = jnp.dot(full_one, pre_one_grad, preferred_element_type=jnp.float32)
    star_grad = star_grad + input_grad[:levels]
    stored_grad = jnp.take(star_grad, level_order, axis=0)
    pressure_new = forward_slabs[0]
    wind_new = forward_slabs[1]
    pressure_grad = lax.all_to_all(
        stored_grad[None].astype(jnp.bfloat16), "slab", split_axis=1, concat_axis=2, tiled=True
    ).astype(jnp.float32)[0]
    return (pressure_new, wind_new, pressure_grad, first_grad, second_grad, third_grad)


def solution(mesh):
    in_specs = (
        P("slab", "date"),
        P("slab", "date"),
        P("slab", "date"),
        P(None, "slab", "date"),
        P(),
        P(),
        P(),
        P(),
        P(),
        P("slab", None),
        P("slab", None),
        P("slab", None),
        P("slab", "date"),
        P("slab", "date"),
    )
    out_specs = (
        P("slab", "date"),
        P("slab", "date"),
        P("slab", "date"),
        P(("date", "slab"), None),
        P(("date", "slab"), None),
        P(("date", "slab"), None),
    )
    return jax.shard_map(body, mesh=mesh, in_specs=in_specs, out_specs=out_specs, check_vma=False)
```

profile of v0, /device:TPU:0, one launch (start us, length us, event | category | flops | bytes accessed | tf_op | source)
XLA Modules:
  0.0 540.4 jit_solution(8033137742579381662)
XLA Ops:
  7.2 1.2 fusion.38
  8.4 0.8 fusion.39
  9.1 34.3 %gather_fusion.4 = f32[6144]{0:T(1024)S(1)} fusion(f32[6144]{0:T(1024)S(1)} %bitcast.140, s32[6144]{0:T(1024)S(1)} %fusion.25), kind=kCustom, calls=%fused_computation.3.clone | custom fusion | bytes 73728 | tf_op jit(solution)/shard_map/jit(_take)/gather | solution.py:64
  43.5 34.3 %gather_fusion.5 = f32[6144]{0:T(1024)S(1)} fusion(f32[6144]{0:T(1024)S(1)} %bitcast.141, s32[6144]{0:T(1024)S(1)} %fusion.26), kind=kCustom, calls=%fused_computation.4.clone | custom fusion | bytes 73728 | tf_op jit(solution)/shard_map/jit(_take)/gather | solution.py:65
  77.8 34.3 %gather_fusion.2 = f32[6144]{0:T(1024)S(1)} fusion(f32[6144]{0:T(1024)S(1)} %bitcast.138, s32[6144]{0:T(1024)S(1)} %fusion.23), kind=kCustom, calls=%fused_computation.clone | custom fusion | bytes 73728 | tf_op jit(solution)/shard_map/jit(_take)/gather | solution.py:62
  112.2 34.3 %gather_fusion.3 = f32[6144]{0:T(1024)S(1)} fusion(f32[6144]{0:T(1024)S(1)} %bitcast.139, s32[6144]{0:T(1024)S(1)} %fusion.24), kind=kCustom, calls=%fused_computation.2.clone | custom fusion | bytes 73728 | tf_op jit(solution)/shard_map/jit(_take)/gather | solution.py:63
  146.7 0.2 pad_maximum_fusion
  146.9 4.0 copy.50
  150.9 0.5 broadcast.246
  151.5 34.5 %reduce.6 = bf16[6144,4]{1,0:T(8,128)(2,1)} reduce(bf16[6144,1,4]{2,1,0:T(2,128)(2,1)S(1)} %bitcast.142, bf16[]{:T(256)} %broadcast.246), dimensions={1}, to_apply=%bitcast.107.reduce_sub_computation | reduce | bytes 98306
  186.0 4.4 reshape.350
  190.4 7.4 %all-to-all-start = ((bf16[16,2,768]{2,1,0:T(2,128)(2,1)}), bf16[16,2,768]{2,1,0:T(2,128)(2,1)S(1)}, u32[]{:S(2)}, u32[]{:S(2)}) async-start(bf16[16,2,768]{2,1,0:T(2,128)(2,1)} %reshape.350), calls=%async_computation | async-start | bytes 98304 | tf_op jit(solution)/shard_map/all_to_all | solution.py:70
  197.8 1.2 sort.17
  199.2 21.9 %all-gather = bf16[16,4,512]{2,1,0:T(4,128)(2,1)S(1)} all-gather(bf16[1,4,512]{2,1,0:T(4,128)(2,1)S(1)} %bitcast.168), channel_id=1, replica_groups=mesh['date'=2,'slab'=16] {'slab'}, dimensions={0}, use_global_device_ids=true | all-gather | bytes 69632 | tf_op jit(solution)/shard_map/all_gather | solution.py:78
  221.1 20.3 %all_gather.10 = bf16[512,512]{1,0:T(8,128)(2,1)} all-gather(bf16[32,512]{1,0:T(8,128)(2,1)S(1)} %copy-done.2), channel_id=1, replica_groups=mesh['date'=2,'slab'=16] {'slab'}, dimensions={0}, use_global_device_ids=true | all-gather | bytes 557056 | tf_op jit(solution)/shard_map/all_gather | solution.py:79
  241.4 19.3 %all-gather.1 = bf16[16,32,16]{1,2,0:T(8,128)(2,1)S(1)} all-gather(bf16[1,32,16]{1,2,0:T(8,128)(2,1)S(1)} %bitcast.169), channel_id=1, replica_groups=mesh['date'=2,'slab'=16] {'slab'}, dimensions={0}, use_global_device_ids=true | all-gather | bytes 17408 | tf_op jit(solution)/shard_map/all_gather | solution.py:80
  261.0 1.4 cholesky.17
  262.5 0.6 compare_reduce_fusion
  263.1 0.6 fusion.28
  263.8 1.2 custom-call.10
  265.0 0.2 fusion.31
  265.2 0.1 fusion.29
  265.4 3.3 copy.56
  268.7 0.5 broadcast.247
  269.2 28.4 %reduce.7 = f32[6144,2]{1,0:T(8,128)} reduce(f32[6144,1,2]{2,1,0:T(1,128)S(1)} %bitcast.143, f32[]{:T(128)} %broadcast.247), dimensions={1}, to_apply=%bitcast.109.reduce_sub_computation | reduce | bytes 98308
  297.6 4.3 reshape.352
  302.0 3.5 all-to-all-start.2
  305.5 0.3 reduce-scatter.7.cloned.1.call-start
  305.7 4.0 reshape.351
  309.7 2.9 copy.51
  312.7 0.6 gather_fusion
  313.4 0.8 reduce.8
  314.2 4.5 reshape.353
  318.7 1.2 copy.58
  319.9 0.6 gather_fusion.7
  320.7 0.3 convolution_tanh_fusion.1
  321.0 1.4 convolution_tanh_fusion
  322.4 0.2 fusion.2
  322.7 0.2 fusion.41
  322.9 0.2 broadcast_multiply_fusion
  323.1 0.2 convolution_multiply_fusion.4
  323.3 0.3 fusion.1
  323.6 0.8 copy.63
  324.5 0.4 fusion
  324.9 0.8 convolution_multiply_fusion.3
  325.8 1.4 convolution_multiply_fusion
  327.3 0.3 convolution_bitcast_fusion
  327.6 0.6 gather_fusion.1
  328.3 0.7 reduce.9
  329.0 0.7 reshape.354
  329.7 6.0 %all-to-all-start.3 = ((bf16[16,2,192]{2,1,0:T(2,128)(2,1)}), bf16[16,2,192]{2,1,0:T(2,128)(2,1)S(1)}, u32[]{:S(2)}, u32[]{:S(2)}) async-start(bf16[16,2,192]{2,1,0:T(2,128)(2,1)} %reshape.354), calls=%async_computation.3 | async-start | bytes 32768 | tf_op jit(solution)/shard_map/all_to_all | solution.py:131
  335.7 0.6 gather_fusion.6
  336.3 0.7 bitcast_convert_fusion
  337.0 5.1 all-to-all-done.3
  342.2 3.5 all-to-all-start.1
  345.7 0.6 dynamic-slice
  347.0 0.6 convert.31
  347.7 4.5 all-to-all-done.1
  352.2 0.7 fusion.40
  352.8 28.3 %reduce-scatter.7.cloned.1.call-done = f32[32,16]{1,0:T(8,128)} async-done(((f32[512,16]{1,0:T(8,128)}), f32[32,16]{1,0:T(8,128)}) %reduce-scatter.7.cloned.1.call-update) | async-done | bytes 2064
  381.1 1.4 copy.64
  382.5 88.1 %all-reduce.6.cloned.1.call-done = f32[64,512]{1,0:T(8,128)} async-done(((f32[64,512]{1,0:T(8,128)}), f32[64,512]{1,0:T(8,128)}) %all-reduce.6.cloned.1.call-update) | async-done | bytes 131088
  470.6 1.3 constant_dynamic-slice_fusion
  472.0 61.9 %reduce-scatter.5.cloned.1.call-done = f32[32,512]{1,0:T(8,128)} async-done(((f32[512,512]{1,0:T(8,128)}), f32[32,512]{1,0:T(8,128)}) %reduce-scatter.5.cloned.1.call-update) | async-done | bytes 65552 | tf_op jit(solution)/shard_map/reduce_scatter | solution.py:123
  (81 shorter events, 1.5 us)
Async XLA Ops:
  112.1 34.4 %copy-start.4 = (f32[1,6144]{1,0:T(1,128)S(1)}, f32[1,6144]{1,0:T(1,128)}, u32[]{:S(2)}) copy-start(f32[1,6144]{1,0:T(1,128)} %param.19) | copy-start | bytes 73732
  112.1 34.4 %copy-start.1 = (f32[2,6144]{1,0:T(2,128)S(1)}, f32[2,6144]{1,0:T(2,128)}, u32[]{:S(2)}) copy-start(f32[2,6144]{1,0:T(2,128)} %param.22) | copy-start | bytes 147460
  112.1 34.4 %copy-start.3 = (f32[1,6144]{1,0:T(1,128)S(1)}, f32[1,6144]{1,0:T(1,128)}, u32[]{:S(2)}) copy-start(f32[1,6144]{1,0:T(1,128)} %param.18) | copy-start | bytes 73732
  112.1 34.5 %copy-start.5 = (f32[1,6144]{1,0:T(1,128)S(1)}, f32[1,6144]{1,0:T(1,128)}, u32[]{:S(2)}) copy-start(f32[1,6144]{1,0:T(1,128)} %param.20) | copy-start | bytes 73732
  151.4 46.3 %copy-start.13 = (s32[16]{0:T(128)S(1)}, s32[16]{0:T(128)}, u32[]{:S(2)}) copy-start(s32[16]{0:T(128)} %param.24) | copy-start | bytes 196
  151.5 47.7 %copy-start.8 = (bf16[4,512]{1,0:T(4,128)(2,1)S(1)}, bf16[4,512]{1,0:T(4,128)(2,1)}, u32[]{:S(2)}) copy-start(bf16[4,512]{1,0:T(4,128)(2,1)} %param.27) | copy-start | bytes 12292
  151.5 69.6 %copy-start.2 = (bf16[32,512]{1,0:T(8,128)(2,1)S(1)}, bf16[32,512]{1,0:T(8,128)(2,1)}, u32[]{:S(2)}) copy-start(bf16[32,512]{1,0:T(8,128)(2,1)} %param.28) | copy-start | bytes 98308
  151.5 89.9 %copy-start.9 = (bf16[32,16]{0,1:T(8,128)(2,1)S(1)}, bf16[32,16]{0,1:T(8,128)(2,1)}, u32[]{:S(2)}) copy-start(bf16[32,16]{0,1:T(8,128)(2,1)} %param.29) | copy-start | bytes 3076
  151.5 109.3 %copy-start.10 = (f32[16]{0:T(128)S(1)}, f32[16]{0:T(128)}, u32[]{:S(2)}) copy-start(f32[16]{0:T(128)} %param.25) | copy-start | bytes 196
  151.5 109.3 %copy-start.12 = (pred[16]{0:T(512)(128)(4,1)S(1)}, pred[16]{0:T(512)(128)(4,1)}, u32[]{:S(2)}) copy-start(pred[16]{0:T(512)(128)(4,1)} %constant.116.clone.1) | copy-start | bytes 52
  151.5 113.9 %copy-start.6 = (f32[1,6144]{1,0:T(1,128)S(1)}, f32[1,6144]{1,0:T(1,128)}, u32[]{:S(2)}) copy-start(f32[1,6144]{1,0:T(1,128)} %param.31) | copy-start | bytes 73732
  151.5 113.9 %copy-start.7 = (f32[1,6144]{1,0:T(1,128)S(1)}, f32[1,6144]{1,0:T(1,128)}, u32[]{:S(2)}) copy-start(f32[1,6144]{1,0:T(1,128)} %param.30) | copy-start | bytes 73732
  190.4 111.6 %all-to-all-start = ((bf16[16,2,768]{2,1,0:T(2,128)(2,1)}), bf16[16,2,768]{2,1,0:T(2,128)(2,1)S(1)}, u32[]{:S(2)}, u32[]{:S(2)}) async-start(bf16[16,2,768]{2,1,0:T(2,128)(2,1)} %reshape.350), calls=%async_computation | async-start | bytes 98304 | tf_op jit(solution)/shard_map/all_to_all | solution.py:70
  302.0 11.4 %all-to-all-start.2 = ((f32[16,1,768]{2,1,0:T(1,128)}), f32[16,1,768]{2,1,0:T(1,128)S(1)}, u32[]{:S(2)}, u32[]{:S(2)}) async-start(f32[16,1,768]{2,1,0:T(1,128)} %reshape.352), calls=%async_computation.2 | async-start | bytes 98304 | tf_op jit(solution)/shard_map/all_to_all | solution.py:106
  305.5 75.7 %reduce-scatter.7.cloned.1.call-start = ((), (), s32[]{:S(2)}) async-start(), calls=%async_computation.7 | async-start | bytes 278528
  318.7 3.7 copy-start.11
  320.7 3.8 copy-start
  324.4 146.2 %all-reduce.6.cloned.1.call-start = ((), (), s32[]{:S(2)}) async-start(), calls=%async_computation.8 | async-start | bytes 262144
  324.9 20.8 %copy-start.14 = (u32[32]{0:T(128)S(1)}, u32[32]{0:T(128)}, u32[]{:S(2)}) copy-start(u32[32]{0:T(128)} %constant.136) | copy-start | bytes 388
  325.8 208.2 %reduce-scatter.5.cloned.1.call-start = ((), (), s32[]{:S(2)}) async-start(), calls=%async_computation.6 | async-start | bytes 1114112 | tf_op jit(solution)/shard_map/reduce_scatter | solution.py:123
  329.7 12.5 %all-to-all-start.3 = ((bf16[16,2,192]{2,1,0:T(2,128)(2,1)}), bf16[16,2,192]{2,1,0:T(2,128)(2,1)S(1)}, u32[]{:S(2)}, u32[]{:S(2)}) async-start(bf16[16,2,192]{2,1,0:T(2,128)(2,1)} %reshape.354), calls=%async_computation.3 | async-start | bytes 32768 | tf_op jit(solution)/shard_map/all_to_all | solution.py:131
  342.2 10.0 %all-to-all-start.1 = ((bf16[2,16,384]{2,0,1:T(2,128)(2,1)}), bf16[2,16,384]{2,0,1:T(2,128)(2,1)S(1)}, u32[]{:S(2)}, u32[]{:S(2)}) async-start(bf16[2,16,384]{2,0,1:T(2,128)(2,1)} %bitcast_convert_fusion), calls=%async_computation.1 | async-start | bytes 49152 | tf_op jit(solution)/shard_map/all_to_all | solution.py:99
Sparse Core Ops, SparseCore 0:
  324.5 56.5 reduce-scatter.6
  384.6 86.0 all-reduce.5
  474.8 59.0 reduce-scatter.4
where the time goes:
time: 541 us; the launch traced here: 540 us
  waiting for transfers between devices  188 us (35%)
  local copies, waits for them, and re-layouts  177 us (33%)
  other arithmetic  72 us (13%)
  blocking collectives  61.4 us (11%)
  starting transfers between devices  20.7 us (4%)
  between operations  15 us (3%)
  matrix products  6.09 us (1%)
    unnamed x5, waiting for transfers between devices  116 us
    unnamed x3, other arithmetic  63.6 us
    reduce_scatter x1, waiting for transfers between devices, body(): lax.psum_scatter(local_two, 'slab', scatter_dimension=0, tiled=True)  61.9 us
    gather x1, local copies, waits for them, and re-layouts, body(): south = jnp.take(horizontal_wind[1], neighbors[3], axis=1)  34.3 us
    gather x1, local copies, waits for them, and re-layouts, body(): east = jnp.take(horizontal_wind[0], neighbors[0], axis=1)  34.3 us
    gather x1, local copies, waits for them, and re-layouts, body(): west = jnp.take(horizontal_wind[0], neighbors[1], axis=1)  34.3 us
    gather x1, local copies, waits for them, and re-layouts, body(): north = jnp.take(horizontal_wind[1], neighbors[2], axis=1)  34.3 us
    unnamed x44, local copies, waits for them, and re-layouts  23.4 us
  transfers between devices with their start and end apart: 7, of which 5 were waited for; matrix products, arithmetic and copies ran while one was open for 11% of the time, Pallas kernels for 0%

commit v1 on v0

--- a/solution.py
+++ b/solution.py
@@ -128,8 +128,16 @@
     stored_grad = jnp.take(star_grad, level_order, axis=0)
     pressure_new = forward_slabs[0]
     wind_new = forward_slabs[1]
-    pressure_grad = lax.all_to_all(
-        stored_grad[None].astype(jnp.bfloat16), "slab", split_axis=1, concat_axis=2, tiled=True
+    pressure_grad = jnp.concatenate(
+        lax.all_to_all(
+            jnp.stack(
+                jnp.split(stored_grad[None].astype(jnp.bfloat16), lax.axis_size("slab"), axis=1)
+            ),
+            "slab",
+            0,
+            0,
+        ),
+        axis=2,
     ).astype(jnp.float32)[0]
     return (pressure_new, wind_new, pressure_grad, first_grad, second_grad, third_grad)
 

time: 541 us -> 547 us (1.011)
    unnamed x3 -> x2, other arithmetic: 63.6 us -> 62.8 us
    unnamed x44 -> x71, local copies, waits for them, and re-layouts: 23.4 us -> 23.6 us
where the time goes in v1:
time: 547 us; the launch traced here: 546 us
  waiting for transfers between devices  191 us (35%)
  local copies, waits for them, and re-layouts  178 us (33%)
  other arithmetic  73.4 us (13%)
  blocking collectives  61.4 us (11%)
  starting transfers between devices  20.7 us (4%)
  between operations  15 us (3%)
  matrix products  6.11 us (1%)
    unnamed x5, waiting for transfers between devices  119 us
    unnamed x2, other arithmetic  62.8 us
    reduce_scatter x1, waiting for transfers between devices, body(): lax.psum_scatter(local_two, 'slab', scatter_dimension=0, tiled=True)  61.9 us
    gather x1, local copies, waits for them, and re-layouts, body(): east = jnp.take(horizontal_wind[0], neighbors[0], axis=1)  34.3 us
    gather x1, local copies, waits for them, and re-layouts, body(): west = jnp.take(horizontal_wind[0], neighbors[1], axis=1)  34.3 us
    gather x1, local copies, waits for them, and re-layouts, body(): north = jnp.take(horizontal_wind[1], neighbors[2], axis=1)  34.3 us
    gather x1, local copies, waits for them, and re-layouts, body(): south = jnp.take(horizontal_wind[1], neighbors[3], axis=1)  34.3 us
    unnamed x71, local copies, waits for them, and re-layouts  23.6 us
  transfers between devices with their start and end apart: 7, of which 5 were waited for; matrix products, arithmetic and copies ran while one was open for 11% of the time, Pallas kernels for 0%

profile of v1, /device:TPU:0, one launch (start us, length us, event | category | flops | bytes accessed | tf_op | source)
XLA Modules:
  0.0 545.8 jit_solution(1739755569360778780)
XLA Ops:
  7.2 1.2 fusion.38
  8.4 0.8 fusion.39
  9.1 34.3 %gather_fusion.4 = f32[6144]{0:T(1024)S(1)} fusion(f32[6144]{0:T(1024)S(1)} %bitcast.201, s32[6144]{0:T(1024)S(1)} %get-tuple-element.30), kind=kCustom, calls=%fused_computation.3.clone | custom fusion | bytes 73728 | tf_op jit(solution)/shard_map/jit(_take)/gather | solution.py:64
  43.4 34.3 %gather_fusion.5 = f32[6144]{0:T(1024)S(1)} fusion(f32[6144]{0:T(1024)S(1)} %bitcast.202, s32[6144]{0:T(1024)S(1)} %get-tuple-element.31), kind=kCustom, calls=%fused_computation.4.clone | custom fusion | bytes 73728 | tf_op jit(solution)/shard_map/jit(_take)/gather | solution.py:65
  77.8 34.3 %gather_fusion.2 = f32[6144]{0:T(1024)S(1)} fusion(f32[6144]{0:T(1024)S(1)} %bitcast.199, s32[6144]{0:T(1024)S(1)} %get-tuple-element.28), kind=kCustom, calls=%fused_computation.clone | custom fusion | bytes 73728 | tf_op jit(solution)/shard_map/jit(_take)/gather | solution.py:62
  112.1 34.3 %gather_fusion.3 = f32[6144]{0:T(1024)S(1)} fusion(f32[6144]{0:T(1024)S(1)} %bitcast.200, s32[6144]{0:T(1024)S(1)} %get-tuple-element.29), kind=kCustom, calls=%fused_computation.2.clone | custom fusion | bytes 73728 | tf_op jit(solution)/shard_map/jit(_take)/gather | solution.py:63
  146.8 4.0 copy.48
  150.9 0.5 broadcast.246
  151.4 34.5 %reduce.6 = bf16[6144,4]{1,0:T(8,128)(2,1)} reduce(bf16[6144,1,4]{2,1,0:T(2,128)(2,1)S(1)} %bitcast.203, bf16[]{:T(256)} %broadcast.246), dimensions={1}, to_apply=%bitcast.171.reduce_sub_computation | reduce | bytes 98306
  186.0 4.4 reshape.348
  190.3 7.4 %all-to-all-start = ((bf16[16,2,768]{2,1,0:T(2,128)(2,1)}), bf16[16,2,768]{2,1,0:T(2,128)(2,1)S(1)}, u32[]{:S(2)}, u32[]{:S(2)}) async-start(bf16[16,2,768]{2,1,0:T(2,128)(2,1)} %reshape.348), calls=%async_computation | async-start | bytes 98304 | tf_op jit(solution)/shard_map/all_to_all | solution.py:70
  197.7 1.2 sort.17
  199.0 0.5 compare_and_fusion
  199.6 0.6 broadcast_in_dim.111
  200.2 21.9 %all-gather = bf16[16,4,512]{2,1,0:T(4,128)(2,1)S(1)} all-gather(bf16[1,4,512]{2,1,0:T(4,128)(2,1)S(1)} %bitcast.229), channel_id=1, replica_groups=mesh['date'=2,'slab'=16] {'slab'}, dimensions={0}, use_global_device_ids=true | all-gather | bytes 69632 | tf_op jit(solution)/shard_map/all_gather | solution.py:78
  222.1 20.3 %all_gather.10 = bf16[512,512]{1,0:T(8,128)(2,1)} all-gather(bf16[32,512]{1,0:T(8,128)(2,1)S(1)} %copy-done.2), channel_id=1, replica_groups=mesh['date'=2,'slab'=16] {'slab'}, dimensions={0}, use_global_device_ids=true | all-gather | bytes 557056 | tf_op jit(solution)/shard_map/all_gather | solution.py:79
  242.3 19.3 %all-gather.1 = bf16[16,32,16]{1,2,0:T(8,128)(2,1)S(1)} all-gather(bf16[1,32,16]{1,2,0:T(8,128)(2,1)S(1)} %bitcast.230), channel_id=1, replica_groups=mesh['date'=2,'slab'=16] {'slab'}, dimensions={0}, use_global_device_ids=true | all-gather | bytes 17408 | tf_op jit(solution)/shard_map/all_gather | solution.py:80
  262.0 1.4 cholesky.17
  263.5 0.6 compare_reduce_fusion
  264.1 0.6 fusion.28
  264.8 1.2 custom-call.10
  266.4 3.3 copy.54
  269.7 0.5 broadcast.247
  270.2 28.3 %reduce.7 = f32[6144,2]{1,0:T(8,128)} reduce(f32[6144,1,2]{2,1,0:T(1,128)S(1)} %bitcast.204, f32[]{:T(128)} %broadcast.247), dimensions={1}, to_apply=%bitcast.173.reduce_sub_computation | reduce | bytes 98308
  298.5 4.3 reshape.350
  302.8 0.6 pad_clamp_fusion
  303.4 3.5 all-to-all-start.2
  306.9 0.3 reduce-scatter.7.cloned.1.call-start
  307.2 4.0 reshape.349
  311.1 2.9 copy.49
  314.1 0.6 gather_fusion
  314.8 0.6 fusion.36
  315.4 0.7 reduce.8
  316.1 4.5 reshape.351
  320.7 1.2 copy.56
  321.9 0.9 gather_fusion.7
  322.9 0.3 convolution_tanh_fusion.1
  323.2 1.4 convolution_tanh_fusion
  324.7 0.2 fusion.2
  325.1 0.2 broadcast_multiply_fusion
  325.5 0.3 fusion.1
  325.8 1.5 convolution_multiply_fusion
  327.3 0.4 fusion
  327.7 0.8 convolution_multiply_fusion.3
  328.5 0.3 convolution_bitcast_fusion
  328.8 0.9 copy.60
  329.8 0.7 gather_fusion.1
  330.8 0.7 reduce-scatter.5.cloned.1.call-update
  331.5 0.7 reduce.9
  332.3 0.7 reshape.352
  332.9 6.0 %all-to-all-start.3 = ((bf16[16,2,192]{2,1,0:T(2,128)(2,1)}), bf16[16,2,192]{2,1,0:T(2,128)(2,1)S(1)}, u32[]{:S(2)}, u32[]{:S(2)}) async-start(bf16[16,2,192]{2,1,0:T(2,128)(2,1)} %reshape.352), calls=%async_computation.3 | async-start | bytes 32768 | tf_op jit(solution)/shard_map/all_to_all | solution.py:132
  339.0 0.7 gather_fusion.6
  339.7 0.7 bitcast_convert_fusion
  340.4 5.0 all-to-all-done.3
  345.4 3.5 all-to-all-start.1
  348.9 0.6 dynamic-slice
  350.3 0.6 convert.31
  350.9 4.5 all-to-all-done.1
  355.5 0.7 fusion.40
  356.1 30.3 %reduce-scatter.7.cloned.1.call-done = f32[32,16]{1,0:T(8,128)} async-done(((f32[512,16]{1,0:T(8,128)}), f32[32,16]{1,0:T(8,128)}) %reduce-scatter.7.cloned.1.call-update) | async-done | bytes 2064
  386.5 1.4 copy.61
  387.8 88.1 %all-reduce.6.cloned.1.call-done = f32[64,512]{1,0:T(8,128)} async-done(((f32[64,512]{1,0:T(8,128)}), f32[64,512]{1,0:T(8,128)}) %all-reduce.6.cloned.1.call-update) | async-done | bytes 131088
  476.0 1.3 constant_dynamic-slice_fusion
  477.3 61.9 %reduce-scatter.5.cloned.1.call-done = f32[32,512]{1,0:T(8,128)} async-done(((f32[512,512]{1,0:T(8,128)}), f32[32,512]{1,0:T(8,128)}) %reduce-scatter.5.cloned.1.call-update) | async-done | bytes 65552 | tf_op jit(solution)/shard_map/reduce_scatter | solution.py:123
  (104 shorter events, 2.4 us)
Async XLA Ops:
  112.1 34.4 %copy-start.4 = (f32[1,6144]{1,0:T(1,128)S(1)}, f32[1,6144]{1,0:T(1,128)}, u32[]{:S(2)}) copy-start(f32[1,6144]{1,0:T(1,128)} %param.20) | copy-start | bytes 73732
  112.1 34.4 %copy-start.5 = (f32[1,6144]{1,0:T(1,128)S(1)}, f32[1,6144]{1,0:T(1,128)}, u32[]{:S(2)}) copy-start(f32[1,6144]{1,0:T(1,128)} %param.19) | copy-start | bytes 73732
  112.1 34.4 %copy-start.1 = (f32[2,6144]{1,0:T(2,128)S(1)}, f32[2,6144]{1,0:T(2,128)}, u32[]{:S(2)}) copy-start(f32[2,6144]{1,0:T(2,128)} %param.22) | copy-start | bytes 147460
  112.1 34.4 %copy-start.3 = (f32[1,6144]{1,0:T(1,128)S(1)}, f32[1,6144]{1,0:T(1,128)}, u32[]{:S(2)}) copy-start(f32[1,6144]{1,0:T(1,128)} %param.18) | copy-start | bytes 73732
  151.4 46.3 %copy-start.19 = (s32[16]{0:T(128)S(1)}, s32[16]{0:T(128)}, u32[]{:S(2)}) copy-start(s32[16]{0:T(128)} %param.24) | copy-start | bytes 196
  151.4 48.8 %copy-start.10 = (bf16[4,512]{1,0:T(4,128)(2,1)S(1)}, bf16[4,512]{1,0:T(4,128)(2,1)}, u32[]{:S(2)}) copy-start(bf16[4,512]{1,0:T(4,128)(2,1)} %param.27) | copy-start | bytes 12292
  151.4 70.7 %copy-start.2 = (bf16[32,512]{1,0:T(8,128)(2,1)S(1)}, bf16[32,512]{1,0:T(8,128)(2,1)}, u32[]{:S(2)}) copy-start(bf16[32,512]{1,0:T(8,128)(2,1)} %param.28) | copy-start | bytes 98308
  151.4 90.9 %copy-start.11 = (bf16[32,16]{0,1:T(8,128)(2,1)S(1)}, bf16[32,16]{0,1:T(8,128)(2,1)}, u32[]{:S(2)}) copy-start(bf16[32,16]{0,1:T(8,128)(2,1)} %param.29) | copy-start | bytes 3076
  151.4 110.4 %copy-start.15 = (f32[16]{0:T(128)S(1)}, f32[16]{0:T(128)}, u32[]{:S(2)}) copy-start(f32[16]{0:T(128)} %param.25) | copy-start | bytes 196
  151.4 110.4 %copy-start.18 = (pred[16]{0:T(512)(128)(4,1)S(1)}, pred[16]{0:T(512)(128)(4,1)}, u32[]{:S(2)}) copy-start(pred[16]{0:T(512)(128)(4,1)} %constant.116.clone.1) | copy-start | bytes 52
  151.4 114.9 %copy-start.6 = (f32[1,6144]{1,0:T(1,128)S(1)}, f32[1,6144]{1,0:T(1,128)}, u32[]{:S(2)}) copy-start(f32[1,6144]{1,0:T(1,128)} %param.31) | copy-start | bytes 73732
  151.4 114.9 %copy-start.7 = (f32[1,6144]{1,0:T(1,128)S(1)}, f32[1,6144]{1,0:T(1,128)}, u32[]{:S(2)}) copy-start(f32[1,6144]{1,0:T(1,128)} %param.30) | copy-start | bytes 73732
  190.3 113.1 %all-to-all-start = ((bf16[16,2,768]{2,1,0:T(2,128)(2,1)}), bf16[16,2,768]{2,1,0:T(2,128)(2,1)S(1)}, u32[]{:S(2)}, u32[]{:S(2)}) async-start(bf16[16,2,768]{2,1,0:T(2,128)(2,1)} %reshape.348), calls=%async_computation | async-start | bytes 98304 | tf_op jit(solution)/shard_map/all_to_all | solution.py:70
  199.0 115.7 %copy-start.12 = (pred[16]{0:T(512)(128)(4,1)}, pred[16]{0:T(512)(128)(4,1)S(1)}, u32[]{:S(2)}) copy-start(pred[16]{0:T(512)(128)(4,1)S(1)} %compare_and_fusion.1) | copy-start | bytes 52
  303.4 10.7 %copy-start.8 = (s32[1024]{0:T(1024)}, s32[1024]{0:T(1024)S(1)}, u32[]{:S(2)}) copy-start(s32[1024]{0:T(1024)S(1)} %get-tuple-element.33) | copy-start | bytes 12292
  303.4 12.0 %all-to-all-start.2 = ((f32[16,1,768]{2,1,0:T(1,128)}), f32[16,1,768]{2,1,0:T(1,128)S(1)}, u32[]{:S(2)}, u32[]{:S(2)}) async-start(f32[16,1,768]{2,1,0:T(1,128)} %reshape.350), calls=%async_computation.2 | async-start | bytes 98304 | tf_op jit(solution)/shard_map/all_to_all | solution.py:106
  306.9 79.5 %reduce-scatter.7.cloned.1.call-start = ((), (), s32[]{:S(2)}) async-start(), calls=%async_computation.7 | async-start | bytes 278528
  316.1 6.6 %copy-start.13 = (pred[16]{0:T(512)(128)(4,1)S(1)}, pred[16]{0:T(512)(128)(4,1)}, u32[]{:S(2)}) copy-start(pred[16]{0:T(512)(128)(4,1)} %copy-done.12) | copy-start | bytes 52
  316.1 6.7 %copy-start.17 = (pred[64]{0:T(512)(128)(4,1)S(1)}, pred[64]{0:T(512)(128)(4,1)}, u32[]{:S(2)}) copy-start(pred[64]{0:T(512)(128)(4,1)} %broadcast_in_dim.111) | copy-start | bytes 196
  321.8 2.8 copy-start.9
  321.9 2.8 copy-start.16
  324.7 2.6 copy-start
  325.8 4.7 copy-start.14
  327.3 21.6 %copy-start.20 = (u32[32]{0:T(128)S(1)}, u32[32]{0:T(128)}, u32[]{:S(2)}) copy-start(u32[32]{0:T(128)} %constant.136) | copy-start | bytes 388
  329.7 146.3 %all-reduce.6.cloned.1.call-start = ((), (), s32[]{:S(2)}) async-start(), calls=%async_computation.8 | async-start | bytes 262144
  330.8 208.5 %reduce-scatter.5.cloned.1.call-start = ((), (), s32[]{:S(2)}) async-start(), calls=%async_computation.6 | async-start | bytes 1114112 | tf_op jit(solution)/shard_map/reduce_scatter | solution.py:123
  332.9 12.5 %all-to-all-start.3 = ((bf16[16,2,192]{2,1,0:T(2,128)(2,1)}), bf16[16,2,192]{2,1,0:T(2,128)(2,1)S(1)}, u32[]{:S(2)}, u32[]{:S(2)}) async-start(bf16[16,2,192]{2,1,0:T(2,128)(2,1)} %reshape.352), calls=%async_computation.3 | async-start | bytes 32768 | tf_op jit(solution)/shard_map/all_to_all | solution.py:132
  345.4 10.0 %all-to-all-start.1 = ((bf16[2,16,384]{2,0,1:T(2,128)(2,1)}), bf16[2,16,384]{2,0,1:T(2,128)(2,1)S(1)}, u32[]{:S(2)}, u32[]{:S(2)}) async-start(bf16[2,16,384]{2,0,1:T(2,128)(2,1)} %bitcast_convert_fusion), calls=%async_computation.1 | async-start | bytes 49152 | tf_op jit(solution)/shard_map/all_to_all | solution.py:99
Sparse Core Ops, SparseCore 0:
  329.8 56.5 reduce-scatter.6
  389.9 86.0 all-reduce.5
  480.2 59.0 reduce-scatter.4
